TPU v7x, 32 devices: a whole 2x2x4 slice. The times are simulated.
32 devices in a mesh: row: 4 (over x, core), col: 2 (over y), depth: 4 (over z).
Axes of the slice: x: 2, y: 2, z: 4, core: 2. Of those that a mesh axis runs over, the one named last changes fastest.
Arguments:
- tokens: bfloat16 [64, 6144], P(('col', 'depth'), 'row'), may hold values from -6 to 6
- first_weight: bfloat16 [6144, 24576], P('row', ('col', 'depth')), may hold values from -0.078125 to 0.078125
- first_tangent: bfloat16 [6144, 24576], P('row', ('col', 'depth')), may hold values from -0.078125 to 0.078125
- second_weight: bfloat16 [24576, 6144], P(('col', 'depth'), 'row'), may hold values from -0.0390625 to 0.0390625
- second_tangent: bfloat16 [24576, 6144], P(('col', 'depth'), 'row'), may hold values from -0.0390625 to 0.0390625
Outputs:
- grad_first: float32 [6144, 24576], P('row', ('col', 'depth'))
- grad_second: float32 [24576, 6144], P(('col', 'depth'), 'row')
All inputs are finite; a program needn't handle non-finite values.
Results may differ from a plain program's by a relative error of at most 0.0047.
Values may be sent and summed in bfloat16 or wider, within the bound.
A program may use at most 192 MiB of HBM per device.

v0:
```python
import math

import jax
import jax.numpy as jnp
from jax import lax
from jax.sharding import PartitionSpec as P


def gelu_parts(hidden, hidden_tan):
    inner = 0.7978845608 * (hidden + 0.044715 * hidden * hidden * hidden)
    tval = jnp.tanh(inner)
    active = (0.5 * hidden * (1.0 + tval)).astype(jnp.bfloat16)
    slopes = 0.5 * (1.0 + tval) + 0.5 * hidden * (1.0 - tval * tval) * 0.7978845608 * (
        1.0 + 3.0 * 0.044715 * hidden * hidden
    )
    active_tan = (slopes * hidden_tan).astype(jnp.bfloat16)
    return (active, active_tan, slopes)


def on_device(tokens, first_weight, first_tangent, second_weight, second_tangent):
    gathered = lax.all_gather(tokens, ("col", "depth"), axis=0, tiled=True)
    hidden = jnp.dot(gathered, first_weight, preferred_element_type=jnp.float32)
    hidden_tan = jnp.dot(gathered, first_tangent, preferred_element_type=jnp.float32)
    hidden, hidden_tan = lax.psum((hidden, hidden_tan), "row")
    active, active_tan, slopes = gelu_parts(hidden, hidden_tan)
    partial_value = jnp.dot(
        active_tan, second_weight, preferred_element_type=jnp.float32
    ) + jnp.dot(active, second_tangent, preferred_element_type=jnp.float32)
    out_tan = lax.psum(partial_value, ("col", "depth")).astype(jnp.bfloat16)
    backward = lax.dot_general(
        out_tan, second_weight, (((1,), (1,)), ((), ())), preferred_element_type=jnp.float32
    )
    backward = lax.psum(backward, "row")
    back_hidden = (backward * slopes).astype(jnp.bfloat16)
    factor = 1.0 / math.sqrt(gathered.shape[0])
    grad_second = (
        lax.dot_general(
            active, out_tan, (((0,), (0,)), ((), ())), preferred_element_type=jnp.float32
        )
        * factor
    )
    grad_first = (
        lax.dot_general(
            gathered, back_hidden, (((0,), (0,)), ((), ())), preferred_element_type=jnp.float32
        )
        * factor
    )
    return (grad_first, grad_second)


def solution(mesh):
    return jax.shard_map(
        on_device,
        mesh=mesh,
        in_specs=(
            P(("col", "depth"), "row"),
            P("row", ("col", "depth")),
            P("row", ("col", "depth")),
            P(("col", "depth"), "row"),
            P(("col", "depth"), "row"),
        ),
        out_specs=(P("row", ("col", "depth")), P(("col", "depth"), "row")),
        check_vma=False,
    )
```

profile of v0, /device:TPU:0, one launch (start us, length us, event | category | flops | bytes accessed | tf_op | source)
XLA Modules:
  0.0 220.9 jit_solution(1123703977794834401)
XLA Ops:
  7.2 0.0 slice-start.3
  7.2 0.0 all-reduce.7.cloned.1.call-start
  7.2 33.1 %all_gather.3 = bf16[64,1536]{1,0:T(8,128)(2,1)S(1)} all-gather(bf16[8,1536]{1,0:T(8,128)(2,1)} %param.5), channel_id=1, replica_groups=mesh['row'=4,'col'=2,'depth'=4] {'col','depth'}, dimensions={0}, use_global_device_ids=true | all-gather | bytes 221184 | tf_op jit(solution)/shard_map/all_gather | solution.py:21
  40.3 0.0 slice-start.4
  40.3 0.0 slice-start.5
  40.3 6.5 %fusion.12 = f32[64,3072]{1,0:T(8,128)} fusion(bf16[64,1536]{1,0:T(8,128)(2,1)S(1)} %all_gather.3, bf16[1536,3072]{1,0:T(8,128)(2,1)} %param.7), kind=kOutput, calls=%fused_computation.18 | convolution fusion | flops 603979776 | bytes 10420224 | tf_op jit(solution)/shard_map/dot_general | solution.py:23
  46.8 0.0 slice-done.3
  46.8 0.0 slice-done.4
  46.8 0.0 slice-done.5
  46.8 2.6 %fusion.11 = f32[64,3072]{1,0:T(8,128)} fusion(bf16[64,1536]{1,0:T(8,128)(2,1)S(1)} %all_gather.3, bf16[1536,3072]{1,0:T(8,128)(2,1)S(1)} %bitcast.15), kind=kOutput, calls=%fused_computation.17 | convolution fusion | flops 603979776 | bytes 10420224 | tf_op jit(solution)/shard_map/dot_general | solution.py:22
  49.4 0.0 slice-start
  49.4 0.0 all-reduce.7.cloned.1.call-update
  49.5 0.0 all-reduce.5.cloned.1.call-start
  49.5 44.0 %all-reduce.7.cloned.1.call-done = (f32[64,3072]{1,0:T(8,128)}, f32[64,3072]{1,0:T(8,128)}) async-done(((f32[64,3072]{1,0:T(8,128)}, f32[64,3072]{1,0:T(8,128)}), (f32[64,3072]{1,0:T(8,128)}, f32[64,3072]{1,0:T(8,128)})) %all-reduce.7.cloned.1.call-update) | async-done | bytes 1572880 | tf_op jit(solution)/shard_map/psum | solution.py:24
  93.5 0.0 slice-start.1
  93.5 0.0 slice-start.2
  93.5 0.0 copy-start
  93.5 6.3 %fusion.5 = f32[64,1536]{1,0:T(8,128)S(1)} fusion(bf16[3072,1536]{1,0:T(8,128)(2,1)} %param.8, f32[64,3072]{1,0:T(8,128)} %get-tuple-element.4, f32[64,3072]{1,0:T(8,128)} %get-tuple-element.5), kind=kOutput, calls=%fused_computation.13 | convolution fusion | flops 607715328 | bytes 11403264 | tf_op jit(solution)/shard_map/dot_general | solution.py:26
  99.8 0.0 slice-done
  99.8 0.0 slice-done.1
  99.8 0.3 slice-done.2
  100.1 0.1 copy-done
  100.2 1.8 convolution_add_fusion
  102.0 44.5 %all-reduce.8 = bf16[64,1536]{1,0:T(8,128)(2,1)S(1)} all-reduce(f32[64,1536]{1,0:T(8,128)S(1)} %convolution_add_fusion), channel_id=1, replica_groups=mesh['row'=4,'col'=2,'depth'=4] {'col','depth'}, use_global_device_ids=true, to_apply=%region_2.0 | all-reduce | flops 98304 | bytes 589824 | tf_op jit(solution)/shard_map/psum | solution.py:29
  146.5 7.5 %fusion.13 = f32[64,3072]{1,0:T(8,128)} fusion(bf16[64,1536]{1,0:T(8,128)(2,1)S(1)} %all-reduce.8, bf16[3072,1536]{1,0:T(8,128)(2,1)} %param.8), kind=kOutput, calls=%fused_computation.19 | convolution fusion | flops 603979776 | bytes 10420224 | tf_op jit(solution)/shard_map/dot_general | solution.py:30
  154.0 0.0 all-reduce.5.cloned.1.call-update
  154.0 8.3 %convolution_multiply_fusion = f32[3072,1536]{1,0:T(8,128)} fusion(bf16[64,1536]{1,0:T(8,128)(2,1)S(1)} %all-reduce.8, f32[64,3072]{1,0:T(8,128)S(1)} %copy-done), kind=kOutput, calls=%fused_computation.1 | convolution fusion | flops 610467840 | bytes 19857408 | tf_op jit(solution)/shard_map/dot_general | solution.py:37
  162.3 23.6 %all-reduce.5.cloned.1.call-done = f32[64,3072]{1,0:T(8,128)} async-done(((f32[64,3072]{1,0:T(8,128)}), f32[64,3072]{1,0:T(8,128)}) %all-reduce.5.cloned.1.call-update) | async-done | bytes 786448 | tf_op jit(solution)/shard_map/psum | solution.py:33
  185.9 9.6 %multiply_bitcast_fusion = f32[1536,3072]{0,1:T(8,128)} fusion(bf16[64,1536]{1,0:T(8,128)(2,1)S(1)} %all_gather.3, f32[64,3072]{1,0:T(8,128)} %all-reduce.5.cloned.1.call-done, f32[64,3072]{1,0:T(8,128)S(1)} %copy-done), kind=kOutput, calls=%fused_computation | convolution fusion | flops 612433920 | bytes 20643840 | tf_op jit(solution)/shard_map/dot_general | solution.py:43
  195.4 18.6 %copy.7 = f32[1536,3072]{1,0:T(8,128)} copy(f32[1536,3072]{0,1:T(8,128)} %multiply_bitcast_fusion) | data formatting | bytes 37748736
  (2 shorter events, 0.0 us)
Async XLA Ops:
  7.2 39.6 %slice-start.3 = ((s8[9437184]{0:T(1024)(128)(4,1)}), s8[1048576]{0:T(1024)(128)(4,1)S(1)}, s32[]{:S(2)}) async-start(s8[9437184]{0:T(1024)(128)(4,1)} %bitcast.14), calls=%async_computation.5 | async-start | bytes 2097152
  7.2 86.3 %all-reduce.7.cloned.1.call-start = ((), (), s32[]{:S(2)}) async-start(), calls=%async_computation.1 | async-start | bytes 3145728 | tf_op jit(solution)/shard_map/psum | solution.py:24
  40.3 6.5 %slice-start.4 = ((s8[9437184]{0:T(1024)(128)(4,1)}), s8[4194304]{0:T(1024)(128)(4,1)S(1)}, s32[]{:S(2)}) async-start(s8[9437184]{0:T(1024)(128)(4,1)} %bitcast.14), calls=%async_computation.6 | async-start | bytes 8388608
  40.3 6.5 %slice-start.5 = ((s8[9437184]{0:T(1024)(128)(4,1)}), s8[4194304]{0:T(1024)(128)(4,1)S(1)}, s32[]{:S(2)}) async-start(s8[9437184]{0:T(1024)(128)(4,1)} %bitcast.14), calls=%async_computation.7 | async-start | bytes 8388608
  49.4 50.3 %slice-start = ((s8[9437184]{0:T(1024)(128)(4,1)}), s8[1048576]{0:T(1024)(128)(4,1)S(1)}, s32[]{:S(2)}) async-start(s8[9437184]{0:T(1024)(128)(4,1)} %bitcast.12), calls=%async_computation.2 | async-start | bytes 2097152
  49.5 136.4 %all-reduce.5.cloned.1.call-start = ((), (), s32[]{:S(2)}) async-start(), calls=%async_computation | async-start | bytes 1572864 | tf_op jit(solution)/shard_map/psum | solution.py:33
  93.5 6.3 %slice-start.1 = ((s8[9437184]{0:T(1024)(128)(4,1)}), s8[4194304]{0:T(1024)(128)(4,1)S(1)}, s32[]{:S(2)}) async-start(s8[9437184]{0:T(1024)(128)(4,1)} %bitcast.12), calls=%async_computation.3 | async-start | bytes 8388608
  93.5 6.6 %slice-start.2 = ((s8[9437184]{0:T(1024)(128)(4,1)}), s8[4194304]{0:T(1024)(128)(4,1)S(1)}, s32[]{:S(2)}) async-start(s8[9437184]{0:T(1024)(128)(4,1)} %bitcast.12), calls=%async_computation.4 | async-start | bytes 8388608
  93.5 6.7 %copy-start = (f32[64,3072]{1,0:T(8,128)S(1)}, f32[64,3072]{1,0:T(8,128)}, u32[]{:S(2)}) copy-start(f32[64,3072]{1,0:T(8,128)} %get-tuple-element.5) | copy-start | bytes 2359300
Sparse Core Ops, SparseCore 0:
  49.6 43.8 all-reduce.6
  154.1 31.7 all-reduce.4
where the time goes:
time: 221 us
  blocking collectives  77.6 us (35%)
  waiting for transfers between devices  67.6 us (31%)
  matrix products  42.5 us (19%)
  local copies, waits for them, and re-layouts  19.1 us (9%)
  between operations  14.1 us (6%)
    psum x1, blocking collectives, on_device(): out_tan = lax.psum(partial_value, ('col', 'depth')).astype(jnp.bfloat16)  44.5 us
    psum x1, waiting for transfers between devices, on_device(): hidden, hidden_tan = lax.psum((hidden, hidden_tan), 'row')  44 us
    all_gather x1, blocking collectives, on_device(): gathered = lax.all_gather(tokens, ('col', 'depth'), axis=0, tiled=True)  33.1 us
    psum x1, waiting for transfers between devices, on_device(): backward = lax.psum(backward, 'row')  23.6 us
    unnamed x15, local copies, waits for them, and re-layouts  19.1 us
    dot_general x1, matrix products, on_device(): lax.dot_general(gathered, back_hidden, (((0,), (0,)), ((), ())), preferre...  9.56 us
    dot_general x1, matrix products, on_device(): lax.dot_general(active, out_tan, (((0,), (0,)), ((), ())), preferred_elem...  8.3 us
    dot_general x1, matrix products, on_device(): lax.dot_general(out_tan, second_weight, (((1,), (1,)), ((), ())), preferr...  7.5 us
  transfers between devices with their start and end apart: 2, of which 2 were waited for; matrix products, arithmetic and copies ran while one was open for 4% of the time, Pallas kernels for 0%

commit v1 on v0

v1 whole, which is shorter than its diff:
```python
import functools
import math

import jax
import jax.numpy as jnp
from jax import lax
from jax.experimental import pallas as pl
from jax.experimental.pallas import tpu as pltpu
from jax.sharding import PartitionSpec as P

CORES = 2
LANES = 128
F32 = jnp.float32
BF16 = jnp.bfloat16


def pieces(extent, most):
    return max(n for n in range(1, most + 1) if extent % (n * LANES) == 0)


def gelu_parts(hidden, hidden_tan):
    inner = 0.7978845608 * (hidden + 0.044715 * hidden * hidden * hidden)
    tval = jnp.tanh(inner)
    active = 0.5 * hidden * (1.0 + tval)
    slopes = 0.5 * (1.0 + tval) + 0.5 * hidden * (1.0 - tval * tval) * 0.7978845608 * (
        1.0 + 3.0 * 0.044715 * hidden * hidden
    )
    return active, slopes * hidden_tan, slopes


def block_kernel(
    sizes,
    tok_ref, fw_ref, ft_ref, sw_ref, st_ref,
    tok_out, act_out, tan_out, back_out,
    w1, w2, tokg, tok2d, hbuf, psend, precv, xsend, xrecv, acts, slopes,
    acc, rsend, rrecv, outg, bsend, brecv, bxsend, bxrecv, back,
    wsem, tok_s, tok_r, ps, pr, xs, xr, as_, ar, rs, rr, gs, gr, bps, bpr, bxs, bxr, bas, bar_,
):
    chips, ncol, ndepth, nf, no = sizes
    group = ncol * ndepth
    tl, dl = tok_ref.shape
    total = group * tl
    half = total // CORES
    cw = w1.shape[-1]
    dn = dl // no

    row = lax.axis_index("row")
    core = lax.rem(row, CORES)
    chip = lax.div(row, CORES)
    mate = {"row": chip * CORES + (1 - core)}
    across = [{"row": lax.rem(chip + o, chips) * CORES + core} for o in range(1, chips)]
    me = lax.axis_index("col") * ndepth + lax.axis_index("depth")
    ranks = [lax.rem(me + o, group) for o in range(1, group)]
    peers = [{"col": lax.div(r, ndepth), "depth": lax.rem(r, ndepth)} for r in ranks]
    mine = pl.ds(pl.multiple_of(core * half, half), half)
    other = pl.ds(pl.multiple_of((1 - core) * half, half), half)

    loads = {}
    for i, ref in enumerate((fw_ref, ft_ref)):
        for k in range(nf):
            loads[i, k] = pltpu.make_async_copy(
                ref.at[:, pl.ds(k * cw, cw)], w1.at[i, k], wsem.at[i, k]
            )
    for i, ref in enumerate((sw_ref, st_ref)):
        for k in range(nf):
            loads[2 + i, k] = pltpu.make_async_copy(
                ref.at[pl.ds(k * cw, cw), :], w2.at[i, k], wsem.at[2 + i, k]
            )
    for pair in (0, 2):
        for k in range(nf):
            loads[pair, k].start()
            loads[pair + 1, k].start()

    sent = []

    def send(src, dst, ssem, rsem, device):
        copy = pltpu.make_async_remote_copy(
            src_ref=src, dst_ref=dst, send_sem=ssem, recv_sem=rsem,
            device_id=device, device_id_type=pl.DeviceIdType.MESH,
        )
        copy.start()
        sent.append(copy)
        return copy

    barrier = pltpu.get_barrier_semaphore()
    everyone = [mate] + across + peers
    for device in everyone:
        pl.semaphore_signal(
            barrier, inc=1, device_id=device, device_id_type=pl.DeviceIdType.MESH
        )
    pl.semaphore_wait(barrier, len(everyone))

    arrivals = [
        send(tok_ref, tokg.at[me], tok_s.at[o], tok_r.at[o], device)
        for o, device in enumerate(peers)
    ]
    tokg[me] = tok_ref[...]
    for copy in arrivals:
        copy.wait_recv()
    tok2d[...] = tokg[...].astype(F32).reshape(total, dl).astype(BF16)
    tok_out[...] = tok2d[...]

    cols = [pl.ds(k * cw, cw) for k in range(nf)]
    to_mate, to_chips, halves = {}, {}, {}

    def first(k):
        for i in range(2):
            loads[i, k].wait()
            hbuf[i, :, cols[k]] = jnp.dot(tok2d[...], w1[i, k], preferred_element_type=F32)
            psend[k, i] = hbuf[i, other, cols[k]]
        to_mate[k] = send(psend.at[k], precv.at[k], ps.at[k], pr.at[k], mate)

    def chip_sum(k):
        to_mate[k].wait_recv()
        for i in range(2):
            both = hbuf[i, mine, cols[k]] + precv[k, i]
            hbuf[i, mine, cols[k]] = both
            xsend[k, i] = both.astype(BF16)
        to_chips[k] = [
            send(xsend.at[k], xrecv.at[o, k], xs.at[o, k], xr.at[o, k], device)
            for o, device in enumerate(across)
        ]

    def activate(k):
        hidden, hidden_tan = hbuf[0, mine, cols[k]], hbuf[1, mine, cols[k]]
        for o, copy in enumerate(to_chips[k]):
            copy.wait_recv()
            hidden = hidden + xrecv[o, k, 0].astype(F32)
            hidden_tan = hidden_tan + xrecv[o, k, 1].astype(F32)
        active, active_tan, slope = gelu_parts(hidden, hidden_tan)
        acts[k, 0, mine, :] = active_tan.astype(BF16)
        acts[k, 1, mine, :] = active.astype(BF16)
        slopes[:, cols[k]] = slope
        part = acts.at[k, :, mine, :]
        halves[k] = send(part, part, as_.at[k], ar.at[k], mate)

    scatter, gather = {}, {}

    def second(k):
        halves[k].wait_recv()
        for i in range(2):
            loads[2 + i, k].wait()
        for n in range(no):
            part = pl.ds(n * dn, dn)
            term = jnp.dot(acts[k, 0], w2[0, k, :, part], preferred_element_type=F32)
            term += jnp.dot(acts[k, 1], w2[1, k, :, part], preferred_element_type=F32)
            if k > 0:
                term += acc[n]
            acc[n] = term
            if k == nf - 1:
                rsend[n] = term.reshape(group, tl, dn).astype(BF16)
                scatter[n] = [
                    send(rsend.at[n, r], rrecv.at[n, o], rs.at[n, o], rr.at[n, o], device)
                    for o, (r, device) in enumerate(zip(ranks, peers))
                ]

    for t in range(nf + 5):
        for lag, stage in ((0, first), (1, chip_sum), (3, activate), (5, second)):
            if 0 <= t - lag < nf:
                stage(t - lag)

    for n in range(no):
        value = acc[n, pl.ds(pl.multiple_of(me * tl, tl), tl), :]
        for o, copy in enumerate(scatter[n]):
            copy.wait_recv()
            value += rrecv[n, o].astype(F32)
        outg[n, me] = value.astype(BF16)
        gather[n] = [
            send(outg.at[n, me], outg.at[n, me], gs.at[n, o], gr.at[n, o], device)
            for o, device in enumerate(peers)
        ]

    to_mate, to_chips, halves = {}, {}, {}

    def back_chip_sum(k):
        to_mate[k].wait_recv()
        both = hbuf[0, mine, cols[k]] + brecv[k]
        hbuf[0, mine, cols[k]] = both
        bxsend[k] = both.astype(BF16)
        to_chips[k] = [
            send(bxsend.at[k], bxrecv.at[o, k], bxs.at[o, k], bxr.at[o, k], device)
            for o, device in enumerate(across)
        ]

    def back_finish(k):
        value = hbuf[0, mine, cols[k]]
        for o, copy in enumerate(to_chips[k]):
            copy.wait_recv()
            value += bxrecv[o, k].astype(F32)
        back[k, mine, :] = (value * slopes[:, cols[k]]).astype(BF16)
        part = back.at[k, mine, :]
        halves[k] = send(part, part, bas.at[k], bar_.at[k], mate)

    for n in range(no):
        for copy in gather[n]:
            copy.wait_recv()
        part = pl.ds(n * dn, dn)
        tan_out[:, part] = outg[n].astype(F32).reshape(total, dn).astype(BF16)
        for k in range(nf):
            term = lax.dot_general(
                tan_out[:, part], w2[0, k, :, part], (((1,), (1,)), ((), ())),
                preferred_element_type=F32,
            )
            if n > 0:
                term += hbuf[0, :, cols[k]]
            hbuf[0, :, cols[k]] = term
            if n == no - 1:
                bsend[k] = hbuf[0, other, cols[k]]
                to_mate[k] = send(bsend.at[k], brecv.at[k], bps.at[k], bpr.at[k], mate)
                if k >= 1:
                    back_chip_sum(k - 1)
                if k >= 3:
                    back_finish(k - 3)
    back_chip_sum(nf - 1)
    for k in range(max(0, nf - 3), nf):
        back_finish(k)
    for k in range(nf):
        act_out[k] = acts[k, 1]
    for k in range(nf):
        halves[k].wait_recv()
        back_out[k] = back[k]
    for copy in sent:
        copy.wait_send()


def grads_kernel(factor, tok_ref, act_ref, tan_ref, back_ref, first_ref, second_ref):
    lhs_rows = (((0,), (0,)), ((), ()))
    second_ref[...] = (
        lax.dot_general(act_ref[0], tan_ref[...], lhs_rows, preferred_element_type=F32) * factor
    )
    first_ref[...] = (
        lax.dot_general(tok_ref[...], back_ref[0], lhs_rows, preferred_element_type=F32) * factor
    )


def on_device(axes, tokens, first_weight, first_tangent, second_weight, second_tangent):
    tl, dl = tokens.shape
    fl = first_weight.shape[1]
    ncol, ndepth, chips = axes["col"], axes["depth"], axes["row"] // CORES
    group = ncol * ndepth
    total, half = group * tl, group * tl // CORES
    nf, no = pieces(fl, 6), pieces(dl, 2)
    cw, dn = fl // nf, dl // no
    far = max(chips - 1, 1)
    dma = pltpu.SemaphoreType.DMA
    whole = pl.BlockSpec(memory_space=pltpu.VMEM)
    hbm = pl.BlockSpec(memory_space=pl.ANY)
    gathered, active, out_tan, back_hidden = pl.pallas_call(
        functools.partial(block_kernel, (chips, ncol, ndepth, nf, no)),
        name="block",
        out_shape=(
            jax.ShapeDtypeStruct((total, dl), BF16),
            jax.ShapeDtypeStruct((nf, total, cw), BF16),
            jax.ShapeDtypeStruct((total, dl), BF16),
            jax.ShapeDtypeStruct((nf, total, cw), BF16),
        ),
        in_specs=[whole, hbm, hbm, hbm, hbm],
        out_specs=(whole,) * 4,
        scratch_shapes=[
            pltpu.VMEM((2, nf, dl, cw), BF16),
            pltpu.VMEM((2, nf, cw, dl), BF16),
            pltpu.VMEM((group, tl, dl), BF16),
            pltpu.VMEM((total, dl), BF16),
            pltpu.VMEM((2, total, fl), F32),
            pltpu.VMEM((nf, 2, half, cw), F32),
            pltpu.VMEM((nf, 2, half, cw), F32),
            pltpu.VMEM((nf, 2, half, cw), BF16),
            pltpu.VMEM((far, nf, 2, half, cw), BF16),
            pltpu.VMEM((nf, 2, total, cw), BF16),
            pltpu.VMEM((half, fl), F32),
            pltpu.VMEM((no, total, dn), F32),
            pltpu.VMEM((no, group, tl, dn), BF16),
            pltpu.VMEM((no, group - 1, tl, dn), BF16),
            pltpu.VMEM((no, group, tl, dn), BF16),
            pltpu.VMEM((nf, half, cw), F32),
            pltpu.VMEM((nf, half, cw), F32),
            pltpu.VMEM((nf, half, cw), BF16),
            pltpu.VMEM((far, nf, half, cw), BF16),
            pltpu.VMEM((nf, total, cw), BF16),
            dma((4, nf)),
            dma((group - 1,)), dma((group - 1,)),
            dma((nf,)), dma((nf,)),
            dma((far, nf)), dma((far, nf)),
            dma((nf,)), dma((nf,)),
            dma((no, group - 1)), dma((no, group - 1)),
            dma((no, group - 1)), dma((no, group - 1)),
            dma((nf,)), dma((nf,)),
            dma((far, nf)), dma((far, nf)),
            dma((nf,)), dma((nf,)),
        ],
        compiler_params=pltpu.CompilerParams(
            collective_id=0, has_side_effects=True, vmem_limit_bytes=62 * 1024 * 1024
        ),
    )(tokens, first_weight, first_tangent, second_weight, second_tangent)

    return pl.pallas_call(
        functools.partial(grads_kernel, 1.0 / math.sqrt(total)),
        name="grads",
        grid=(nf,),
        out_shape=(
            jax.ShapeDtypeStruct((dl, fl), F32),
            jax.ShapeDtypeStruct((fl, dl), F32),
        ),
        in_specs=[
            pl.BlockSpec((total, dl), lambda k: (0, 0)),
            pl.BlockSpec((1, total, cw), lambda k: (k, 0, 0)),
            pl.BlockSpec((total, dl), lambda k: (0, 0)),
            pl.BlockSpec((1, total, cw), lambda k: (k, 0, 0)),
        ],
        out_specs=(
            pl.BlockSpec((dl, cw), lambda k: (0, k)),
            pl.BlockSpec((cw, dl), lambda k: (k, 0)),
        ),
    )(gathered, active, out_tan, back_hidden)


def solution(mesh):
    return jax.shard_map(
        functools.partial(on_device, dict(mesh.shape)),
        mesh=mesh,
        in_specs=(
            P(("col", "depth"), "row"),
            P("row", ("col", "depth")),
            P("row", ("col", "depth")),
            P(("col", "depth"), "row"),
            P(("col", "depth"), "row"),
        ),
        out_specs=(P("row", ("col", "depth")), P(("col", "depth"), "row")),
        check_vma=False,
    )
```

time: 221 us -> 65.5 us (0.30)
  blocking collectives: 77.6 us -> 0 us
  waiting for transfers between devices: 67.6 us -> 0 us
  Pallas kernels: 0 us -> 64.7 us
  matrix products: 42.5 us -> 0 us
  local copies, waits for them, and re-layouts: 19.1 us -> 0 us
  between operations: 14.1 us -> 0.64 us
    psum x2 -> x0, waiting for transfers between devices: 67.6 us -> none  [the longest x1 44 us: on_device(): hidden, hidden_tan = lax.psum((hidden, hidden_tan), 'row')]
    pallas_call x0 -> x2, Pallas kernels: none -> 64.7 us  [the longest x1 50.7 us: on_device(): pl.pallas_call(functools.partial(block_kernel, (chips, ncol, ndepth, nf,...]
    psum x1 -> x0, blocking collectives: 44.5 us -> none  [on_device(): out_tan = lax.psum(partial_value, ('col', 'depth')).astype(jnp.bfloat16)]
    dot_general x7 -> x0, matrix products: 42.5 us -> none  [the longest x1 9.56 us: on_device(): lax.dot_general(gathered, back_hidden, (((0,), (0,)), ((), ())), preferre...]
    all_gather x1 -> x0, blocking collectives: 33.1 us -> none  [on_device(): gathered = lax.all_gather(tokens, ('col', 'depth'), axis=0, tiled=True)]
    unnamed x15 -> x0, local copies, waits for them, and re-layouts: 19.1 us -> none
  transfers between devices with their start and end apart: 2 -> 0, of which waited for: 2 -> 0; matrix products, arithmetic and copies ran while one was open for 4% -> 0% of each run, Pallas kernels for 0% -> 0%
where the time goes in v1:
time: 65.5 us; the launch traced here: 65.3 us
  Pallas kernels  64.7 us (99%)
    pallas_call x1, Pallas kernels, on_device(): pl.pallas_call(functools.partial(block_kernel, (chips, ncol, ndepth, nf,...  50.7 us
    pallas_call x1, Pallas kernels, on_device(): pl.pallas_call(functools.partial(grads_kernel, 1.0 / math.sqrt(total)), n...  14 us

profile of v1, /device:TPU:0, one launch (start us, length us, event | category | flops | bytes accessed | tf_op | source)
XLA Modules:
  0.0 65.3 jit_solution(7517149380081275601)
XLA Ops:
  0.6 50.7 %block.1 = (bf16[64,1536]{1,0:T(8,128)(2,1)}, bf16[6,64,512]{2,1,0:T(8,128)(2,1)}, bf16[64,1536]{1,0:T(8,128)(2,1)}, bf16[6,64,512]{2,1,0:T(8,128)(2,1)}) custom-call(bf16[8,1536]{1,0:T(8,128)(2,1)} %tok_ref.1, bf16[1536,3072]{1,0:T(8,128)(2,1)} %fw_ref.1, bf16[1536,3072]{1,0:T(8,128)(2,1)} %ft_ref.1, bf16[3072,1536]{1,0:T(8,128)(2,1)} %sw_ref.1, ...), custom_call_target="tpu_custom_call" | custom-call | tf_op jit(solution)/shard_map/block/pallas_call | solution.py:248
  51.3 14.0 %grads.1 = (f32[1536,3072]{1,0:T(8,128)}, f32[3072,1536]{1,0:T(8,128)}) custom-call(bf16[64,1536]{1,0:T(8,128)(2,1)} %get-tuple-element.6.tok_ref, bf16[6,64,512]{2,1,0:T(8,128)(2,1)} %get-tuple-element.7.act_ref, bf16[64,1536]{1,0:T(8,128)(2,1)} %get-tuple-element.8.tan_ref, bf16[6,64,512]{2,1,0:T(8,128)(2,1)} %get-tuple-element.9.back_ref), custom_call_target="tpu_custom_call" | custom-call | tf_op jit(solution)/shard_map/grads/pallas_call | solution.py:296

commit v2 on v1

--- a/solution.py
+++ b/solution.py
@@ -154,8 +154,8 @@
                     for o, (r, device) in enumerate(zip(ranks, peers))
                 ]
 
-    for t in range(nf + 5):
-        for lag, stage in ((0, first), (1, chip_sum), (3, activate), (5, second)):
+    for t in range(nf + 6):
+        for lag, stage in ((0, first), (2, chip_sum), (4, activate), (6, second)):
             if 0 <= t - lag < nf:
                 stage(t - lag)
 
@@ -207,12 +207,13 @@
             if n == no - 1:
                 bsend[k] = hbuf[0, other, cols[k]]
                 to_mate[k] = send(bsend.at[k], brecv.at[k], bps.at[k], bpr.at[k], mate)
-                if k >= 1:
-                    back_chip_sum(k - 1)
-                if k >= 3:
-                    back_finish(k - 3)
-    back_chip_sum(nf - 1)
-    for k in range(max(0, nf - 3), nf):
+                if k >= 2:
+                    back_chip_sum(k - 2)
+                if k >= 5:
+                    back_finish(k - 5)
+    for k in range(max(0, nf - 2), nf):
+        back_chip_sum(k)
+    for k in range(max(0, nf - 5), nf):
         back_finish(k)
     for k in range(nf):
         act_out[k] = acts[k, 1]
@@ -239,7 +240,7 @@
     ncol, ndepth, chips = axes["col"], axes["depth"], axes["row"] // CORES
     group = ncol * ndepth
     total, half = group * tl, group * tl // CORES
-    nf, no = pieces(fl, 6), pieces(dl, 2)
+    nf, no = pieces(fl, 6), pieces(dl, 3)
     cw, dn = fl // nf, dl // no
     far = max(chips - 1, 1)
     dma = pltpu.SemaphoreType.DMA

time: 65.5 us -> 64.6 us (0.986)
  Pallas kernels: 64.7 us -> 63.8 us
    pallas_call x1, Pallas kernels: 50.7 us -> 49.9 us  [on_device(): pl.pallas_call(functools.partial(block_kernel, (chips, ncol, ndepth, nf,...]
where the time goes in v2:
time: 64.6 us; the launch traced here: 64.5 us
  Pallas kernels  63.8 us (99%)
    pallas_call x1, Pallas kernels, on_device(): pl.pallas_call(functools.partial(block_kernel, (chips, ncol, ndepth, nf,...  49.9 us
    pallas_call x1, Pallas kernels, on_device(): pl.pallas_call(functools.partial(grads_kernel, 1.0 / math.sqrt(total)), n...  14 us

profile of v2, /device:TPU:0, one launch (start us, length us, event | category | flops | bytes accessed | tf_op | source)
XLA Modules:
  0.0 64.5 jit_solution(4488699409898595669)
XLA Ops:
  0.6 49.9 %block.1 = (bf16[64,1536]{1,0:T(8,128)(2,1)}, bf16[6,64,512]{2,1,0:T(8,128)(2,1)}, bf16[64,1536]{1,0:T(8,128)(2,1)}, bf16[6,64,512]{2,1,0:T(8,128)(2,1)}) custom-call(bf16[8,1536]{1,0:T(8,128)(2,1)} %tok_ref.1, bf16[1536,3072]{1,0:T(8,128)(2,1)} %fw_ref.1, bf16[1536,3072]{1,0:T(8,128)(2,1)} %ft_ref.1, bf16[3072,1536]{1,0:T(8,128)(2,1)} %sw_ref.1, ...), custom_call_target="tpu_custom_call" | custom-call | tf_op jit(solution)/shard_map/block/pallas_call | solution.py:249
  50.5 14.0 %grads.1 = (f32[1536,3072]{1,0:T(8,128)}, f32[3072,1536]{1,0:T(8,128)}) custom-call(bf16[64,1536]{1,0:T(8,128)(2,1)} %get-tuple-element.6.tok_ref, bf16[6,64,512]{2,1,0:T(8,128)(2,1)} %get-tuple-element.7.act_ref, bf16[64,1536]{1,0:T(8,128)(2,1)} %get-tuple-element.8.tan_ref, bf16[6,64,512]{2,1,0:T(8,128)(2,1)} %get-tuple-element.9.back_ref), custom_call_target="tpu_custom_call" | custom-call | tf_op jit(solution)/shard_map/grads/pallas_call | solution.py:297
